TPU v7x, 256 devices: a whole 4x4x8 slice. The times are simulated.
256 devices in a mesh: row: 8 (over x_lo, y), col: 32 (over z, x_hi, core).
Axes of the slice: x: 4 (x_hi: 2, x_lo: 2; x = x_hi * 2 + x_lo), y: 4, z: 8, core: 2. Of those that a mesh axis runs over, the one named last changes fastest.
Arguments:
- amplitudes: bfloat16 [32768, 4096], P('col', 'row'), may hold values from -6 to 6
- integrals: bfloat16 [4096, 8192], P('col', 'row'), may hold values from -0.25 to 0.25
- sym_mask: int32 [32, 64], replicated, may hold values from 0 to 1, as said below
Outputs:
- ladder: bfloat16 [32768, 8192], P('col', 'row')
Inputs may be any that keep to these rules, and one draw needn't show every extreme that they name: sym_mask[k, a] is 1 exactly when cd tile k and ab tile a carry the same one of 8 irreducible representations; among the 8 ab tiles of one index of row, at most 2 carry the same representation.
All inputs are finite; a program needn't handle non-finite values.
Results may differ from a plain program's by a relative error of at most 0.001.
Values may be sent and summed in bfloat16 or wider, within the bound.
No kernel may reach another device: no remote copies, remote signals or barrier semaphores. Data moves between devices by JAX's collectives and lax.ppermute only.
A program may use at most 64 MiB of HBM per device.

v0:
```python
import jax
import jax.numpy as jnp
from jax import lax
from jax.sharding import PartitionSpec as P

TILE = 128
AB_TILES = 8


def shards(amplitudes, integrals, sym_mask):
    row_index = lax.axis_index("row")
    col_index = lax.axis_index("col")
    own_mask = lax.dynamic_slice(sym_mask, (col_index, row_index * AB_TILES), (1, AB_TILES))
    column_mask = jnp.repeat(own_mask[0], TILE).astype(jnp.bfloat16)
    masked = integrals * column_mask[None, :]
    whole_amps = lax.all_gather(amplitudes, "row", axis=1, tiled=True)
    total = jnp.dot(
        whole_amps,
        lax.all_gather(masked, "col", axis=0, tiled=True),
        preferred_element_type=jnp.float32,
    )
    return total.astype(jnp.bfloat16)


def solution(mesh):
    placed = (P("col", "row"), P("col", "row"), P())
    return jax.shard_map(
        shards, mesh=mesh, in_specs=placed, out_specs=P("col", "row"), check_vma=False
    )
```

profile of v0, /device:TPU:64, one launch (start us, length us, event | category | flops | bytes accessed | tf_op | source)
XLA Modules:
  0.0 230.7 jit_solution(11474874311722984410)
XLA Ops:
  6.5 0.0 all-gather.5.cloned.1.call-start
  6.5 0.7 all-gather.5.cloned.1.call-update
  7.3 0.0 all-gather.3.cloned.1.call-start
  7.3 0.8 convert_bitcast_fusion.1
  8.1 0.1 broadcast_bitcast_fusion
  8.2 1.7 broadcast_multiply_fusion
  9.8 0.0 all-gather.3.cloned.1.call-update
  9.8 96.0 %all-gather.5.cloned.1.call-done = bf16[1024,4096]{1,0:T(8,128)(2,1)} async-done(((bf16[1024,512]{1,0:T(8,128)(2,1)}), bf16[1024,4096]{1,0:T(8,128)(2,1)}) %all-gather.5.cloned.1.call-update) | async-done | bytes 8388624 | tf_op jit(solution)/shard_map/all_gather | solution.py:16
  105.9 101.6 %all-gather.3.cloned.1.call-done = bf16[4096,1024]{1,0:T(8,128)(2,1)} async-done(((bf16[128,1024]{1,0:T(8,128)(2,1)}), bf16[4096,1024]{1,0:T(8,128)(2,1)}) %all-gather.3.cloned.1.call-update) | async-done | bytes 8388624 | tf_op jit(solution)/shard_map/all_gather | solution.py:19
  207.5 13.8 %convert_bitcast_fusion = bf16[1024,1024]{0,1:T(8,128)(2,1)S(1)} fusion(bf16[4096,1024]{1,0:T(8,128)(2,1)} %all-gather.3.cloned.1.call-done, bf16[1024,4096]{1,0:T(8,128)(2,1)} %all-gather.5.cloned.1.call-done), kind=kOutput, calls=%fused_computation | convolution fusion | flops 8590983168 | bytes 18874368 | tf_op jit(solution)/shard_map/dot_general | solution.py:17
  221.3 2.6 %copy.4 = bf16[1024,1024]{1,0:T(8,128)(2,1)} copy(bf16[1024,1024]{0,1:T(8,128)(2,1)S(1)} %convert_bitcast_fusion) | data formatting | bytes 4194304 | tf_op jit(solution)/shard_map/convert_element_type | solution.py:22
Async XLA Ops:
  6.5 99.3 %all-gather.5.cloned.1.call-start = ((), (), s32[]{:S(2)}) async-start(), calls=%async_computation.1 | async-start | bytes 9437184 | tf_op jit(solution)/shard_map/all_gather | solution.py:16
  7.3 200.3 %all-gather.3.cloned.1.call-start = ((), (), s32[]{:S(2)}) async-start(), calls=%async_computation | async-start | bytes 8650752 | tf_op jit(solution)/shard_map/all_gather | solution.py:19
Sparse Core Ops, SparseCore 0:
  9.1 96.6 all-gather.4
  108.7 98.8 all-gather.2
where the time goes:
time: 234 us; the launch traced here: 231 us
  waiting for transfers between devices  198 us (85%)
  matrix products  13.8 us (6%)
  between operations  13.4 us (6%)
  local copies, waits for them, and re-layouts  2.64 us (1%)
  other arithmetic  2.44 us (1%)
    all_gather x1, waiting for transfers between devices, shards(): lax.all_gather(masked, 'col', axis=0, tiled=True)  102 us
    all_gather x1, waiting for transfers between devices, shards(): whole_amps = lax.all_gather(amplitudes, 'row', axis=1, tiled=True)  96 us
    dot_general x1, matrix products, shards(): jnp.dot(whole_amps, lax.all_gather(masked, 'col', axis=0, tiled=True), pr...  13.8 us
  transfers between devices with their start and end apart: 2, of which 2 were waited for; matrix products, arithmetic and copies ran while one was open for 1% of the time, Pallas kernels for 0%

commit v1 on v0

v1 whole, which is shorter than its diff:
```python
import jax
import jax.numpy as jnp
from jax import lax
from jax.experimental import pallas as pl
from jax.experimental.pallas import tpu as pltpu
from jax.sharding import PartitionSpec as P

TILE = 128
AB = 8
VMEM = pltpu.VMEM
SMEM = pltpu.SMEM


def spec(space):
    return pl.BlockSpec(memory_space=space)


def row_permute(value, flip):
    return lax.ppermute(value, "row", [(i, i ^ flip) for i in range(8)])


def pack_kernel(where_ref, mask_ref, v_ref, out_ref):
    c, r = where_ref[0], where_ref[1]
    first, last, found = jnp.int32(0), jnp.int32(0), jnp.int32(0)
    for j in range(AB):
        hit = mask_ref[c, r * AB + j] > 0
        first = jnp.where(jnp.logical_and(hit, found == 0), j, first)
        last = jnp.where(hit, j, last)
        found = jnp.where(hit, 1, found)
    zero = jnp.zeros((TILE, TILE), v_ref.dtype)
    one = v_ref[:, pl.ds(pl.multiple_of(first * TILE, TILE), TILE)]
    two = v_ref[:, pl.ds(pl.multiple_of(last * TILE, TILE), TILE)]
    out_ref[:, :TILE] = jnp.where(found > 0, one, zero)
    out_ref[:, TILE:] = jnp.where(jnp.logical_and(found > 0, last != first), two, zero)


def table_kernel(where_ref, mask_ref, out_ref):
    r = where_ref[1]

    @pl.loop(0, 32)
    def _(k):
        first, last = jnp.int32(AB), jnp.int32(0)
        for j in range(AB):
            hit = mask_ref[k, r * AB + j] > 0
            first = jnp.where(hit, jnp.minimum(first, j), first)
            last = jnp.where(hit, j, last)
        first = jnp.where(first == AB, 0, first)
        out_ref[0, k] = first
        out_ref[1, k] = last


def add_block(where_ref, table_ref, mine, other, t_ref, z, acc_ref, rows, base):
    xh = lax.rem(lax.div(where_ref[0], 2), 2)
    co = lax.rem(where_ref[0], 2)
    for t in range(4):
        k = z * 4 + t
        j = lax.rem(xh + (t >> 1), 2)
        own = co == (t & 1)
        slab = jnp.where(own, mine[z, j], other[z, j])
        left = pl.ds(pl.multiple_of(table_ref[0, k] * TILE, TILE), TILE)
        right = pl.ds(pl.multiple_of(table_ref[1, k] * TILE, TILE), TILE)
        for m in range(base, base + rows, 256):
            size = min(256, base + rows - m)
            p = jnp.dot(
                t_ref[m - base : m - base + size, t * TILE : (t + 1) * TILE],
                slab,
                preferred_element_type=jnp.float32,
            )
            acc_ref[m : m + size, left] += p[:, :TILE]
            acc_ref[m : m + size, right] += p[:, TILE:]


def first_kernel(where_ref, table_ref, mine, other, *refs):
    *ts, acc_ref = refs
    acc_ref[...] = jnp.zeros_like(acc_ref)
    for t_ref, flip in zip(ts, (0, 4, 1, 3)):
        add_block(where_ref, table_ref, mine, other, t_ref, where_ref[1] ^ flip, acc_ref, 1024, 0)


def second_kernel(where_ref, table_ref, mine, other, acc_in, *refs):
    *ts, acc_ref = refs
    for t_ref, flip in zip(ts, (7, 5, 2)):
        add_block(where_ref, table_ref, mine, other, t_ref, where_ref[1] ^ flip, acc_ref, 1024, 0)


THIRDS = (352, 336, 336)


def third_kernel(where_ref, table_ref, mine, other, acc_ref, ta, tb, tc, out_ref):
    base = 0
    for t_ref, n in zip((ta, tb, tc), THIRDS):
        add_block(where_ref, table_ref, mine, other, t_ref, where_ref[1] ^ 6, acc_ref, n, base)
        out_ref[base : base + n] = acc_ref[base : base + n].astype(out_ref.dtype)
        base += n


def params():
    return pltpu.CompilerParams(vmem_limit_bytes=40 * 1024 * 1024)


def shards(amps, integrals, sym_mask):
    r, c = lax.axis_index("row"), lax.axis_index("col")
    where = jnp.stack([c, r]).astype(jnp.int32)
    packed = pl.pallas_call(
        pack_kernel,
        in_specs=[spec(SMEM), spec(SMEM), spec(VMEM)],
        out_specs=spec(VMEM),
        out_shape=jax.ShapeDtypeStruct((TILE, 2 * TILE), jnp.bfloat16),
        name="pack",
    )(where, sym_mask, integrals)
    table = pl.pallas_call(
        table_kernel,
        in_specs=[spec(SMEM), spec(SMEM)],
        out_specs=spec(SMEM),
        out_shape=jax.ShapeDtypeStruct((2, 32), jnp.int32),
        name="table",
    )(where, sym_mask)
    across = lax.ppermute(packed, "col", [(i, i ^ 2) for i in range(32)])
    pair = jnp.stack([packed, across])
    groups = [[z * 4 + k for z in range(8)] for k in range(4)]
    mine = lax.all_gather(pair, "col", axis=0, tiled=False, axis_index_groups=groups)
    other = lax.ppermute(mine, "col", [(i, i ^ 1) for i in range(32)])

    p1 = row_permute(amps, 4)
    q1 = row_permute(amps, 1)
    w1 = row_permute(amps, 3)
    pw = row_permute(w1, 4)
    qp = row_permute(p1, 1)
    wq = row_permute(q1, 3)
    a, b, _ = THIRDS
    last = (row_permute(wq[:a], 4), row_permute(pw[a : a + b], 1), row_permute(qp[a + b :], 3))

    acc_shape = jax.ShapeDtypeStruct((1024, 1024), jnp.float32)
    acc = pl.pallas_call(
        first_kernel,
        in_specs=[spec(SMEM), spec(SMEM)] + [spec(VMEM)] * 6,
        out_specs=spec(VMEM),
        out_shape=acc_shape,
        compiler_params=params(),
        cost_estimate=pl.CostEstimate(flops=2 * 1024 * 2048 * 1024, bytes_accessed=1, transcendentals=0),
        name="first",
    )(where, table, mine, other, amps, p1, q1, w1)
    acc = pl.pallas_call(
        second_kernel,
        in_specs=[spec(SMEM), spec(SMEM)] + [spec(VMEM)] * 6,
        out_specs=spec(VMEM),
        out_shape=acc_shape,
        input_output_aliases={4: 0},
        compiler_params=params(),
        cost_estimate=pl.CostEstimate(flops=2 * 1024 * 1536 * 1024, bytes_accessed=1, transcendentals=0),
        name="second",
    )(where, table, mine, other, acc, pw, qp, wq)
    return pl.pallas_call(
        third_kernel,
        in_specs=[spec(SMEM), spec(SMEM)] + [spec(VMEM)] * 6,
        out_specs=spec(VMEM),
        out_shape=jax.ShapeDtypeStruct((1024, 1024), jnp.bfloat16),
        compiler_params=params(),
        name="third",
    )(where, table, mine, other, acc, *last)


def solution(mesh):
    placed = (P("col", "row"), P("col", "row"), P())
    return jax.shard_map(
        shards, mesh=mesh, in_specs=placed, out_specs=P("col", "row"), check_vma=False
    )
```

time: 234 us -> 98.3 us (0.42); the launches traced: 231 us -> 97.4 us
  waiting for transfers between devices: 198 us -> 42.1 us
  Pallas kernels: 0 us -> 20.2 us
  starting transfers between devices: 0.04 us -> 14.7 us
  matrix products: 13.8 us -> 0 us
    all_gather x2 -> x1, waiting for transfers between devices: 198 us -> 9.92 us  [shards(): lax.all_gather(pair, 'col', axis=0, tiled=False, axis_index_groups=groups)]
    ppermute x0 -> x11, waiting for transfers between devices: none -> 32.2 us  [the longest x9 29.2 us: row_permute(): return lax.ppermute(value, 'row', [(i, i ^ flip) for i in range(8)])]
    pallas_call x0 -> x5, Pallas kernels: none -> 20.2 us  [the longest x1 7.21 us: shards(): pl.pallas_call(first_kernel, in_specs=[spec(SMEM), spec(SMEM)] + [spec(VM...]
    ppermute x0 -> x11, starting transfers between devices: none -> 14.7 us  [the longest x9 11.7 us: row_permute(): return lax.ppermute(value, 'row', [(i, i ^ flip) for i in range(8)])]
    dot_general x1 -> x0, matrix products: 13.8 us -> none  [shards(): jnp.dot(whole_amps, lax.all_gather(masked, 'col', axis=0, tiled=True), pr...]
    unnamed x0 -> x8, local copies, waits for them, and re-layouts: none -> 3.73 us
    convert_element_type x2 -> x0, local copies, waits for them, and re-layouts: 2.64 us -> none  [the longest x1 2.56 us: shards(): return total.astype(jnp.bfloat16)]
  transfers between devices with their start and end apart: 2 -> 12, of which waited for: 2 -> 5; matrix products, arithmetic and copies ran while one was open for 1% -> 1% of each run, Pallas kernels for 0% -> 15%
where the time goes in v1:
time: 98.3 us; the launch traced here: 97.4 us
  waiting for transfers between devices  42.1 us (43%)
  Pallas kernels  20.2 us (21%)
  starting transfers between devices  14.7 us (15%)
  between operations  13.5 us (14%)
  local copies, waits for them, and re-layouts  4.78 us (5%)
  other arithmetic  2.1 us (2%)
    ppermute x9, waiting for transfers between devices, row_permute(): return lax.ppermute(value, 'row', [(i, i ^ flip) for i in range(8)])  29.2 us
    ppermute x9, starting transfers between devices, row_permute(): return lax.ppermute(value, 'row', [(i, i ^ flip) for i in range(8)])  11.7 us
    all_gather x1, waiting for transfers between devices, shards(): lax.all_gather(pair, 'col', axis=0, tiled=False, axis_index_groups=groups)  9.92 us
    pallas_call x1, Pallas kernels, shards(): pl.pallas_call(first_kernel, in_specs=[spec(SMEM), spec(SMEM)] + [spec(VM...  7.21 us
    pallas_call x1, Pallas kernels, shards(): pl.pallas_call(second_kernel, in_specs=[spec(SMEM), spec(SMEM)] + [spec(V...  5.19 us
    unnamed x8, local copies, waits for them, and re-layouts  3.73 us
    pallas_call x1, Pallas kernels, shards(): pl.pallas_call(third_kernel, in_specs=[spec(SMEM), spec(SMEM)] + [spec(VM...  3.61 us
    ppermute x1, starting transfers between devices, shards(): across = lax.ppermute(packed, 'col', [(i, i ^ 2) for i in range(32)])  3.02 us
  transfers between devices with their start and end apart: 12, of which 5 were waited for; matrix products, arithmetic and copies ran while one was open for 1% of the time, Pallas kernels for 15%

profile of v1, /device:TPU:64, one launch (start us, length us, event | category | flops | bytes accessed | tf_op | source)
XLA Modules:
  0.0 97.4 jit_solution(3674889823050880215)
XLA Ops:
  6.5 0.0 all-gather.3.cloned.1.call-start
  6.5 0.6 pad_add_fusion.where_ref
  7.1 1.6 %pack.1 = bf16[128,256]{1,0:T(8,128)(2,1)} custom-call(s32[2]{0:T(128)} %pad_add_fusion.where_ref, s32[32,64]{1,0:T(8,128)} %mask_ref.3, bf16[128,1024]{1,0:T(8,128)(2,1)} %v_ref.1), custom_call_target="tpu_custom_call" | custom-call | tf_op jit(solution)/shard_map/pack/pallas_call | solution.py:104
  8.8 3.0 %collective-permute-start = (bf16[128,256]{1,0:T(8,128)(2,1)}, bf16[128,256]{1,0:T(8,128)(2,1)S(1)}, u32[]{:S(2)}, u32[]{:S(2)}) collective-permute-start(bf16[128,256]{1,0:T(8,128)(2,1)} %pack.1), channel_id=1, source_target_pairs={{0,2},{1,3},{2,0},{3,1},{4,6},{5,7},{6,4},{7,5},{8,10},{9,11},{10,... | collective-permute-start | bytes 196616 | tf_op jit(solution)/shard_map/ppermute | solution.py:118
  11.8 3.0 %collective-permute-done = bf16[128,256]{1,0:T(8,128)(2,1)S(1)} collective-permute-done((bf16[128,256]{1,0:T(8,128)(2,1)}, bf16[128,256]{1,0:T(8,128)(2,1)S(1)}, u32[]{:S(2)}, u32[]{:S(2)}) %collective-permute-start) | collective-permute-done | bytes 65568 | tf_op jit(solution)/shard_map/ppermute | solution.py:118
  14.8 1.5 %pad_maximum_fusion = bf16[2,128,256]{2,1,0:T(8,128)(2,1)} fusion(bf16[1,128,256]{2,1,0:T(8,128)(2,1)S(1)} %bitcast.10, bf16[1,128,256]{2,1,0:T(8,128)(2,1)} %bitcast.9), kind=kLoop, calls=%fused_computation | loop fusion | flops 65536 | bytes 262144 | tf_op jit(solution)/shard_map/stack | solution.py:119
  16.3 0.0 all-gather.3.cloned.1.call-update
  16.3 1.7 %collective-permute-start.3 = (bf16[1024,512]{1,0:T(8,128)(2,1)}, bf16[1024,512]{1,0:T(8,128)(2,1)}, u32[]{:S(2)}, u32[]{:S(2)}) collective-permute-start(bf16[1024,512]{1,0:T(8,128)(2,1)} %refs_0_.1), channel_id=1, source_target_pairs={{0,32},{32,0},{64,96},{96,64},{128,160},{160,128},{192,224},{224,1... | collective-permute-start | bytes 3145736 | tf_op jit(solution)/shard_map/ppermute | solution.py:19
  18.0 1.5 %collective-permute-start.2 = (bf16[1024,512]{1,0:T(8,128)(2,1)}, bf16[1024,512]{1,0:T(8,128)(2,1)}, u32[]{:S(2)}, u32[]{:S(2)}) collective-permute-start(bf16[1024,512]{1,0:T(8,128)(2,1)} %refs_0_.1), channel_id=1, source_target_pairs={{0,128},{32,160},{64,192},{96,224},{128,0},{160,32},{192,64},{224,... | collective-permute-start | bytes 3145736 | tf_op jit(solution)/shard_map/ppermute | solution.py:19
  19.4 2.2 %collective-permute-start.4 = (bf16[1024,512]{1,0:T(8,128)(2,1)}, bf16[1024,512]{1,0:T(8,128)(2,1)}, u32[]{:S(2)}, u32[]{:S(2)}) collective-permute-start(bf16[1024,512]{1,0:T(8,128)(2,1)} %refs_0_.1), channel_id=1, source_target_pairs={{0,96},{32,64},{64,32},{96,0},{128,224},{160,192},{192,160},{224,1... | collective-permute-start | bytes 3145736 | tf_op jit(solution)/shard_map/ppermute | solution.py:19
  21.6 18.8 %collective-permute-done.3.refs_2_ = bf16[1024,512]{1,0:T(8,128)(2,1)} collective-permute-done((bf16[1024,512]{1,0:T(8,128)(2,1)}, bf16[1024,512]{1,0:T(8,128)(2,1)}, u32[]{:S(2)}, u32[]{:S(2)}) %collective-permute-start.3) | collective-permute-done | bytes 1048608 | tf_op jit(solution)/shard_map/ppermute | solution.py:19
  40.4 3.0 %collective-permute-start.7 = (bf16[1024,512]{1,0:T(8,128)(2,1)}, bf16[1024,512]{1,0:T(8,128)(2,1)S(1)}, u32[]{:S(2)}, u32[]{:S(2)}) collective-permute-start(bf16[1024,512]{1,0:T(8,128)(2,1)} %collective-permute-done.3.refs_2_), channel_id=1, source_target_pairs={{0,96},{32,64},{64,32},{96,0},{128,224},{160,192},{192,160},{224,1... | collective-permute-start | bytes 3145736 | tf_op jit(solution)/shard_map/ppermute | solution.py:19
  43.5 0.0 collective-permute-done.2.refs_1_
  43.5 0.1 collective-permute-start.6
  43.6 2.3 %collective-permute-done.4.refs_3_ = bf16[1024,512]{1,0:T(8,128)(2,1)} collective-permute-done((bf16[1024,512]{1,0:T(8,128)(2,1)}, bf16[1024,512]{1,0:T(8,128)(2,1)}, u32[]{:S(2)}, u32[]{:S(2)}) %collective-permute-start.4) | collective-permute-done | bytes 1048608 | tf_op jit(solution)/shard_map/ppermute | solution.py:19
  45.9 0.0 collective-permute-start.5
  45.9 9.9 %all-gather.3.cloned.1.call-done = bf16[16,128,256]{2,1,0:T(8,128)(2,1)} async-done(((bf16[2,128,256]{2,1,0:T(8,128)(2,1)}), bf16[16,128,256]{2,1,0:T(8,128)(2,1)}) %all-gather.3.cloned.1.call-update) | async-done | bytes 1048592 | tf_op jit(solution)/shard_map/all_gather | solution.py:121
  55.8 0.0 collective-permute-start.1
  55.8 2.6 %table.1.table_ref = s32[2,32]{1,0:T(2,128)} custom-call(s32[2]{0:T(128)} %pad_add_fusion.where_ref, s32[32,64]{1,0:T(8,128)} %mask_ref.3), custom_call_target="tpu_custom_call" | custom-call | tf_op jit(solution)/shard_map/table/pallas_call | solution.py:111
  58.4 8.1 %collective-permute-done.7.refs_2_ = bf16[1024,512]{1,0:T(8,128)(2,1)S(1)} collective-permute-done((bf16[1024,512]{1,0:T(8,128)(2,1)}, bf16[1024,512]{1,0:T(8,128)(2,1)S(1)}, u32[]{:S(2)}, u32[]{:S(2)}) %collective-permute-start.7) | collective-permute-done | bytes 1048608 | tf_op jit(solution)/shard_map/ppermute | solution.py:19
  66.6 0.6 collective-permute-start.8
  67.2 0.0 collective-permute-done.6.refs_1_
  67.2 2.3 %collective-permute-start.10 = (bf16[336,512]{1,0:T(8,128)(2,1)S(1)}, bf16[336,512]{1,0:T(8,128)(2,1)S(1)}, u32[]{:S(2)}, u32[]{:S(2)}) collective-permute-start(bf16[336,512]{1,0:T(8,128)(2,1)S(1)} %slice.14), channel_id=1, source_target_pairs={{0,96},{32,64},{64,32},{96,0},{128,224},{160,192},{192,160},{224,1... | collective-permute-start | bytes 1032200 | tf_op jit(solution)/shard_map/ppermute | solution.py:19
  69.5 0.0 collective-permute-done.5.refs_0_
  69.5 1.0 %slice.13 = bf16[336,512]{1,0:T(8,128)(2,1)S(1)} slice(bf16[1024,512]{1,0:T(8,128)(2,1)} %collective-permute-done.5.refs_0_), slice={[352:688], [0:512]} | slice | bytes 688128 | tf_op jit(solution)/shard_map/slice | solution.py:131
  70.5 0.3 collective-permute-start.9
  70.8 0.0 collective-permute-done.1.other
  70.8 0.0 copy-start
  70.8 1.2 %copy-done = bf16[16,128,256]{2,1,0:T(8,128)(2,1)S(1)} copy-done((bf16[16,128,256]{2,1,0:T(8,128)(2,1)S(1)}, bf16[16,128,256]{2,1,0:T(8,128)(2,1)}, u32[]{:S(2)}) %copy-start) | copy-done | bytes 1048600
  72.0 0.0 copy-start.1
  72.0 0.7 copy-done.1
  72.7 0.0 copy-start.2
  72.7 0.6 copy-done.2
  73.3 0.0 copy-start.3
  73.3 1.2 %copy-done.3 = bf16[1024,512]{1,0:T(8,128)(2,1)S(1)} copy-done((bf16[1024,512]{1,0:T(8,128)(2,1)S(1)}, bf16[1024,512]{1,0:T(8,128)(2,1)}, u32[]{:S(2)}) %copy-start.3) | copy-done | bytes 1048600
  74.5 7.2 %first.1.acc_in = f32[1024,1024]{1,0:T(8,128)S(1)} custom-call(s32[2]{0:T(128)S(1)} %copy-done.2, s32[2,32]{1,0:T(2,128)S(1)} %copy-done.1, bf16[8,2,128,256]{3,2,1,0:T(8,128)(2,1)S(1)} %bitcast.6, bf16[8,2,128,256]{3,2,1,0:T(8,128)(2,1)S(1)} %collective-permute-done.1.other, bf16[1024,512]{1,0:T(8,128)(2,1)S(1)} %copy-done.3, ...), custom_call_target="tpu_custom_call" | custom-call | flops 4294967296 | bytes 1 | tf_op jit(solution)/shard_map/first/pallas_call | solution.py:134
  81.7 5.2 %second.1.acc_ref = f32[1024,1024]{1,0:T(8,128)S(1)} custom-call(s32[2]{0:T(128)S(1)} %copy-done.2, s32[2,32]{1,0:T(2,128)S(1)} %copy-done.1, bf16[8,2,128,256]{3,2,1,0:T(8,128)(2,1)S(1)} %bitcast.7, bf16[8,2,128,256]{3,2,1,0:T(8,128)(2,1)S(1)} %collective-permute-done.1.other, f32[1024,1024]{1,0:T(8,128)S(1)} %first.1.acc_in, ...), custom_call_target="tpu_custom_call", output_to_operand_aliasing={{}: (4, {})} | custom-call | flops 3221225472 | bytes 1 | tf_op jit(solution)/shard_map/second/pallas_call | solution.py:143
  86.9 0.0 collective-permute-done.10.tc
  86.9 0.0 collective-permute-done.9.tb
  86.9 0.0 collective-permute-done.8.ta
  87.0 3.6 %third.1 = bf16[1024,1024]{1,0:T(8,128)(2,1)} custom-call(s32[2]{0:T(128)S(1)} %copy-done.2, s32[2,32]{1,0:T(2,128)S(1)} %copy-done.1, bf16[8,2,128,256]{3,2,1,0:T(8,128)(2,1)S(1)} %bitcast.8, bf16[8,2,128,256]{3,2,1,0:T(8,128)(2,1)S(1)} %collective-permute-done.1.other, f32[1024,1024]{1,0:T(8,128)S(1)} %second.1.acc_ref, ...), custom_call_target="tpu_custom_call" | custom-call | tf_op jit(solution)/shard_map/third/pallas_call | solution.py:153
  (2 shorter events, 0.0 us)
Async XLA Ops:
  6.5 49.3 %all-gather.3.cloned.1.call-start = ((), (), s32[]{:S(2)}) async-start(), calls=%async_computation | async-start | bytes 1179648 | tf_op jit(solution)/shard_map/all_gather | solution.py:121
  8.8 6.0 %collective-permute-start = (bf16[128,256]{1,0:T(8,128)(2,1)}, bf16[128,256]{1,0:T(8,128)(2,1)S(1)}, u32[]{:S(2)}, u32[]{:S(2)}) collective-permute-start(bf16[128,256]{1,0:T(8,128)(2,1)} %pack.1), channel_id=1, source_target_pairs={{0,2},{1,3},{2,0},{3,1},{4,6},{5,7},{6,4},{7,5},{8,10},{9,11},{10,... | collective-permute-start | bytes 196616 | tf_op jit(solution)/shard_map/ppermute | solution.py:118
  16.3 24.2 %collective-permute-start.3 = (bf16[1024,512]{1,0:T(8,128)(2,1)}, bf16[1024,512]{1,0:T(8,128)(2,1)}, u32[]{:S(2)}, u32[]{:S(2)}) collective-permute-start(bf16[1024,512]{1,0:T(8,128)(2,1)} %refs_0_.1), channel_id=1, source_target_pairs={{0,32},{32,0},{64,96},{96,64},{128,160},{160,128},{192,224},{224,1... | collective-permute-start | bytes 3145736 | tf_op jit(solution)/shard_map/ppermute | solution.py:19
  18.0 25.5 %collective-permute-start.2 = (bf16[1024,512]{1,0:T(8,128)(2,1)}, bf16[1024,512]{1,0:T(8,128)(2,1)}, u32[]{:S(2)}, u32[]{:S(2)}) collective-permute-start(bf16[1024,512]{1,0:T(8,128)(2,1)} %refs_0_.1), channel_id=1, source_target_pairs={{0,128},{32,160},{64,192},{96,224},{128,0},{160,32},{192,64},{224,... | collective-permute-start | bytes 3145736 | tf_op jit(solution)/shard_map/ppermute | solution.py:19
  19.4 26.4 %collective-permute-start.4 = (bf16[1024,512]{1,0:T(8,128)(2,1)}, bf16[1024,512]{1,0:T(8,128)(2,1)}, u32[]{:S(2)}, u32[]{:S(2)}) collective-permute-start(bf16[1024,512]{1,0:T(8,128)(2,1)} %refs_0_.1), channel_id=1, source_target_pairs={{0,96},{32,64},{64,32},{96,0},{128,224},{160,192},{192,160},{224,1... | collective-permute-start | bytes 3145736 | tf_op jit(solution)/shard_map/ppermute | solution.py:19
  40.4 26.1 %collective-permute-start.7 = (bf16[1024,512]{1,0:T(8,128)(2,1)}, bf16[1024,512]{1,0:T(8,128)(2,1)S(1)}, u32[]{:S(2)}, u32[]{:S(2)}) collective-permute-start(bf16[1024,512]{1,0:T(8,128)(2,1)} %collective-permute-done.3.refs_2_), channel_id=1, source_target_pairs={{0,96},{32,64},{64,32},{96,0},{128,224},{160,192},{192,160},{224,1... | collective-permute-start | bytes 3145736 | tf_op jit(solution)/shard_map/ppermute | solution.py:19
  43.5 23.7 %collective-permute-start.6 = (bf16[1024,512]{1,0:T(8,128)(2,1)}, bf16[1024,512]{1,0:T(8,128)(2,1)S(1)}, u32[]{:S(2)}, u32[]{:S(2)}) collective-permute-start(bf16[1024,512]{1,0:T(8,128)(2,1)} %collective-permute-done.2.refs_1_), channel_id=1, source_target_pairs={{0,32},{32,0},{64,96},{96,64},{128,160},{160,128},{192,224},{224,1... | collective-permute-start | bytes 3145736 | tf_op jit(solution)/shard_map/ppermute | solution.py:19
  45.9 23.6 %collective-permute-start.5 = (bf16[1024,512]{1,0:T(8,128)(2,1)}, bf16[1024,512]{1,0:T(8,128)(2,1)}, u32[]{:S(2)}, u32[]{:S(2)}) collective-permute-start(bf16[1024,512]{1,0:T(8,128)(2,1)} %collective-permute-done.4.refs_3_), channel_id=1, source_target_pairs={{0,128},{32,160},{64,192},{96,224},{128,0},{160,32},{192,64},{224,... | collective-permute-start | bytes 3145736 | tf_op jit(solution)/shard_map/ppermute | solution.py:19
  55.8 15.0 %collective-permute-start.1 = (bf16[8,2,128,256]{3,2,1,0:T(8,128)(2,1)}, bf16[8,2,128,256]{3,2,1,0:T(8,128)(2,1)S(1)}, u32[]{:S(2)}, u32[]{:S(2)}) collective-permute-start(bf16[8,2,128,256]{3,2,1,0:T(8,128)(2,1)} %bitcast.5), channel_id=1, source_target_pairs={{0,1},{1,0},{2,3},{3,2},{4,5},{5,4},{6,7},{7,6},{8,9},{9,8},{10,11... | collective-permute-start | bytes 3145736 | tf_op jit(solution)/shard_map/ppermute | solution.py:122
  66.6 20.4 %collective-permute-start.8 = (bf16[352,512]{1,0:T(8,128)(2,1)S(1)}, bf16[352,512]{1,0:T(8,128)(2,1)S(1)}, u32[]{:S(2)}, u32[]{:S(2)}) collective-permute-start(bf16[352,512]{1,0:T(8,128)(2,1)S(1)} %slice.12), channel_id=1, source_target_pairs={{0,128},{32,160},{64,192},{96,224},{128,0},{160,32},{192,64},{224,... | collective-permute-start | bytes 1081352 | tf_op jit(solution)/shard_map/ppermute | solution.py:19
  67.2 19.7 %collective-permute-start.10 = (bf16[336,512]{1,0:T(8,128)(2,1)S(1)}, bf16[336,512]{1,0:T(8,128)(2,1)S(1)}, u32[]{:S(2)}, u32[]{:S(2)}) collective-permute-start(bf16[336,512]{1,0:T(8,128)(2,1)S(1)} %slice.14), channel_id=1, source_target_pairs={{0,96},{32,64},{64,32},{96,0},{128,224},{160,192},{192,160},{224,1... | collective-permute-start | bytes 1032200 | tf_op jit(solution)/shard_map/ppermute | solution.py:19
  70.5 16.5 %collective-permute-start.9 = (bf16[336,512]{1,0:T(8,128)(2,1)S(1)}, bf16[336,512]{1,0:T(8,128)(2,1)S(1)}, u32[]{:S(2)}, u32[]{:S(2)}) collective-permute-start(bf16[336,512]{1,0:T(8,128)(2,1)S(1)} %slice.13), channel_id=1, source_target_pairs={{0,32},{32,0},{64,96},{96,64},{128,160},{160,128},{192,224},{224,1... | collective-permute-start | bytes 1032200 | tf_op jit(solution)/shard_map/ppermute | solution.py:19
  70.8 1.2 %copy-start = (bf16[16,128,256]{2,1,0:T(8,128)(2,1)S(1)}, bf16[16,128,256]{2,1,0:T(8,128)(2,1)}, u32[]{:S(2)}) copy-start(bf16[16,128,256]{2,1,0:T(8,128)(2,1)} %all-gather.3.cloned.1.call-done) | copy-start | bytes 3145732
  72.0 0.7 copy-start.1
  72.7 0.6 copy-start.2
  73.3 1.2 %copy-start.3 = (bf16[1024,512]{1,0:T(8,128)(2,1)S(1)}, bf16[1024,512]{1,0:T(8,128)(2,1)}, u32[]{:S(2)}) copy-start(bf16[1024,512]{1,0:T(8,128)(2,1)} %refs_0_.1) | copy-start | bytes 3145732
Sparse Core Ops, SparseCore 0:
  16.4 39.3 all-gather.2
